TPU v7x, 32 devices: a whole 2x2x4 slice. The times are simulated.
32 devices in a mesh: rows: 8 (over z, y), rhs: 4 (over x, core).
Axes of the slice: x: 2, y: 2, z: 4, core: 2. Of those that a mesh axis runs over, the one named last changes fastest.
Arguments:
- rhs: float32 [8192, 2048], P('rows', 'rhs'), parts along dimension 1, may hold values from -6 to 6
- leaf_inverse: float32 [8192, 1024], P('rows'), may hold values from -0.1875 to 0.1875
- basis_left: float32 [3, 8192, 128], P(None, 'rows'), may hold values from -0.5 to 0.5
- basis_right: float32 [3, 8192, 128], P(None, 'rows'), may hold values from -0.09375 to 0.09375
- cores: float32 [7, 256, 256], replicated, may hold values from -0.375 to 0.375
Outputs:
- solution: float32 [8192, 2048], P('rows', 'rhs'), parts along dimension 1
There are 4 independent parts, one for each index of `rhs`. A program takes and returns all parts, laid end to end along the dimension named above; an argument that names none is the same for every part. Nothing has to cross between parts.
All inputs are finite; a program needn't handle non-finite values.
Results may differ from a plain program's by a relative error of at most 0.00011.
Values sent between devices are 32-bit elements; how exact they have to be, the bound alone decides.
A program may use at most 64 MiB of HBM per device.

v0:
```python
import jax
import jax.numpy as jnp
from jax import lax
from jax.sharding import PartitionSpec as P

LEVELS = 3


def swapped(x, axis, apart):
    return lax.ppermute(x, axis, [(i, i ^ 1 << apart) for i in range(lax.axis_size(axis))])


def on_device(rhs, leaf_inverse, basis_left, basis_right, cores):
    highest = lax.Precision.HIGHEST
    current = jnp.dot(leaf_inverse, rhs, precision=highest, preferred_element_type=jnp.float32)
    devices = lax.axis_size("rows")
    tree_depth = devices.bit_length() - 1
    position = lax.axis_index("rows")
    rank_size = basis_left.shape[2]
    for level_index in range(LEVELS, 0, -1):
        span_devices = devices >> level_index
        child_index = position // span_devices
        node_index = child_index // 2
        half_index = child_index % 2
        partial_value = lax.dot_general(
            basis_right[level_index - 1],
            current,
            (((0,), (0,)), ((), ())),
            precision=highest,
            preferred_element_type=jnp.float32,
        )
        child_total = partial_value
        for bit_number in range(tree_depth - level_index):
            child_total = child_total + swapped(child_total, "rows", bit_number)
        sibling = swapped(child_total, "rows", tree_depth - level_index)
        stacked = jnp.where(
            half_index == 0,
            jnp.concatenate([child_total, sibling], axis=0),
            jnp.concatenate([sibling, child_total], axis=0),
        )
        core_block = lax.dynamic_index_in_dim(
            cores, 2 ** (level_index - 1) - 1 + node_index, 0, keepdims=False
        )
        core_rows = lax.dynamic_slice_in_dim(core_block, half_index * rank_size, rank_size, 0)
        coefficients = jnp.dot(
            core_rows, stacked, precision=highest, preferred_element_type=jnp.float32
        )
        current = current - jnp.dot(
            basis_left[level_index - 1],
            coefficients,
            precision=highest,
            preferred_element_type=jnp.float32,
        )
    return current


def solution(mesh):
    placed = (P("rows", "rhs"), P("rows", None), P(None, "rows", None), P(None, "rows", None), P())
    return jax.shard_map(
        on_device, mesh=mesh, in_specs=placed, out_specs=P("rows", "rhs"), check_vma=False
    )
```

profile of v0, /device:TPU:0, one launch (start us, length us, event | category | flops | bytes accessed | tf_op | source)
XLA Modules:
  0.0 85.9 jit_solution(13506359928050524757)
XLA Ops:
  0.0 0.0 copy-start
  0.0 1.6 %copy-done = f32[1024,512]{1,0:T(8,128)S(1)} copy-done((f32[1024,512]{1,0:T(8,128)S(1)}, f32[1024,512]{1,0:T(8,128)}, u32[]{:S(2)}) %copy-start) | copy-done | bytes 2097176
  1.6 8.8 %fusion.45 = f32[1024,512]{1,0:T(8,128)S(1)} fusion(f32[1024,1024]{1,0:T(8,128)} %param.6, f32[1024,512]{1,0:T(8,128)S(1)} %copy-done), kind=kOutput, calls=%fused_computation.54 | convolution fusion | flops 6442450944 | bytes 8388608 | tf_op jit(solution)/shard_map/dot_general | solution.py:15
  10.4 0.0 copy-start.3
  10.4 1.3 %copy-done.3 = f32[1024,512]{1,0:T(8,128)} copy-done((f32[1024,512]{1,0:T(8,128)}, f32[1024,512]{1,0:T(8,128)S(1)}, u32[]{:S(2)}) %copy-start.3) | copy-done | bytes 2097176
  11.7 2.5 %convolution_bitcast_fusion.2 = f32[128,512]{1,0:T(8,128)S(1)} fusion(f32[1024,512]{1,0:T(8,128)S(1)} %fusion.45, f32[3,1024,128]{2,1,0:T(8,128)} %param.8), kind=kOutput, calls=%fused_computation.5 | convolution fusion | flops 805306368 | bytes 2883584 | tf_op jit(solution)/shard_map/dot_general | solution.py:25
  14.2 3.1 %collective-permute-start = (f32[128,512]{1,0:T(8,128)S(1)}, f32[128,512]{1,0:T(8,128)S(1)}, u32[]{:S(2)}, u32[]{:S(2)}) collective-permute-start(f32[128,512]{1,0:T(8,128)S(1)} %convolution_bitcast_fusion.2), channel_id=1, source_target_pairs={{0,4},{4,0},{8,12},{12,8},{16,20},{20,16},{24,28},{28,24},{1,5},{5... | collective-permute-start | bytes 786440 | tf_op jit(solution)/shard_map/ppermute | solution.py:10
  17.3 6.3 %collective-permute-done = f32[128,512]{1,0:T(8,128)S(1)} collective-permute-done((f32[128,512]{1,0:T(8,128)S(1)}, f32[128,512]{1,0:T(8,128)S(1)}, u32[]{:S(2)}, u32[]{:S(2)}) %collective-permute-start) | collective-permute-done | bytes 262176 | tf_op jit(solution)/shard_map/ppermute | solution.py:10
  23.6 1.4 %fusion = f32[128,512]{1,0:T(8,128)S(1)} fusion(f32[128,512]{1,0:T(8,128)S(1)} %collective-permute-done, f32[128,512]{1,0:T(8,128)S(1)} %convolution_bitcast_fusion.2, pred[]{:T(512)S(6)} %eq.13, f32[7,256,256]{2,1,0:T(8,128)} %param.9, s32[]{:T(128)S(6)} %select_n.83, s32[]{:T(128)S(6)} %select_n.86), kind=kOutput, calls=%fused_computation.7 | convolution fusion | flops 201719808 | bytes 917513 | tf_op jit(solution)/shard_map/dot_general | solution.py:45
  25.0 3.6 %bitcast_subtract_fusion.2 = f32[1024,512]{1,0:T(8,128)S(1)} fusion(f32[1024,512]{1,0:T(8,128)} %copy-done.3, f32[128,512]{1,0:T(8,128)S(1)} %fusion, f32[3,1024,128]{2,1,0:T(8,128)} %param.7), kind=kOutput, calls=%fused_computation.2 | convolution fusion | flops 805830656 | bytes 4980736 | tf_op jit(solution)/shard_map/dot_general | solution.py:48
  28.6 0.0 copy-start.2
  28.6 1.3 %copy-done.2 = f32[1024,512]{1,0:T(8,128)} copy-done((f32[1024,512]{1,0:T(8,128)}, f32[1024,512]{1,0:T(8,128)S(1)}, u32[]{:S(2)}) %copy-start.2) | copy-done | bytes 2097176
  29.9 2.5 %convolution_bitcast_fusion.1 = f32[128,512]{1,0:T(8,128)S(1)} fusion(f32[1024,512]{1,0:T(8,128)S(1)} %bitcast_subtract_fusion.2, f32[3,1024,128]{2,1,0:T(8,128)} %param.8), kind=kOutput, calls=%fused_computation.4 | convolution fusion | flops 805306368 | bytes 2883584 | tf_op jit(solution)/shard_map/dot_general | solution.py:25
  32.4 1.8 %collective-permute-start.1 = (f32[128,512]{1,0:T(8,128)S(1)}, f32[128,512]{1,0:T(8,128)S(1)}, u32[]{:S(2)}, u32[]{:S(2)}) collective-permute-start(f32[128,512]{1,0:T(8,128)S(1)} %convolution_bitcast_fusion.1), channel_id=1, source_target_pairs={{0,4},{4,0},{8,12},{12,8},{16,20},{20,16},{24,28},{28,24},{1,5},{5... | collective-permute-start | bytes 786440 | tf_op jit(solution)/shard_map/ppermute | solution.py:10
  34.2 5.7 %collective-permute-done.1 = f32[128,512]{1,0:T(8,128)S(1)} collective-permute-done((f32[128,512]{1,0:T(8,128)S(1)}, f32[128,512]{1,0:T(8,128)S(1)}, u32[]{:S(2)}, u32[]{:S(2)}) %collective-permute-start.1) | collective-permute-done | bytes 262176 | tf_op jit(solution)/shard_map/ppermute | solution.py:10
  39.9 1.6 %collective-permute-start.2 = (f32[128,512]{1,0:T(8,128)S(1)}, f32[128,512]{1,0:T(8,128)S(1)}, u32[]{:S(2)}, u32[]{:S(2)}) collective-permute-start(f32[128,512]{1,0:T(8,128)S(1)} %add.67), channel_id=1, source_target_pairs={{0,8},{4,12},{8,0},{12,4},{16,24},{20,28},{24,16},{28,20},{1,9},{5... | collective-permute-start | bytes 786440 | tf_op jit(solution)/shard_map/ppermute | solution.py:10
  41.5 5.1 %collective-permute-done.2 = f32[128,512]{1,0:T(8,128)S(1)} collective-permute-done((f32[128,512]{1,0:T(8,128)S(1)}, f32[128,512]{1,0:T(8,128)S(1)}, u32[]{:S(2)}, u32[]{:S(2)}) %collective-permute-start.2) | collective-permute-done | bytes 262176 | tf_op jit(solution)/shard_map/ppermute | solution.py:10
  46.6 1.4 %fusion.6 = f32[128,512]{1,0:T(8,128)S(1)} fusion(f32[128,512]{1,0:T(8,128)S(1)} %collective-permute-done.2, f32[128,512]{1,0:T(8,128)S(1)} %add.67, pred[]{:T(512)S(6)} %eq.14, f32[7,256,256]{2,1,0:T(8,128)} %param.9, s32[]{:T(128)S(6)} %select_n.91, s32[]{:T(128)S(6)} %select_n.94), kind=kOutput, calls=%fused_computation.14 | convolution fusion | flops 201719808 | bytes 917513 | tf_op jit(solution)/shard_map/dot_general | solution.py:45
  48.0 3.6 %bitcast_subtract_fusion.1 = f32[1024,512]{1,0:T(8,128)S(1)} fusion(f32[1024,512]{1,0:T(8,128)} %copy-done.2, f32[128,512]{1,0:T(8,128)S(1)} %fusion.6, f32[3,1024,128]{2,1,0:T(8,128)} %param.7), kind=kOutput, calls=%fused_computation.1 | convolution fusion | flops 805830656 | bytes 4980736 | tf_op jit(solution)/shard_map/dot_general | solution.py:48
  51.6 0.0 copy-start.1
  51.6 2.9 %convolution_bitcast_fusion = f32[128,512]{1,0:T(8,128)S(1)} fusion(f32[1024,512]{1,0:T(8,128)S(1)} %bitcast_subtract_fusion.1, f32[3,1024,128]{2,1,0:T(8,128)} %param.8), kind=kOutput, calls=%fused_computation.3 | convolution fusion | flops 805306368 | bytes 2883584 | tf_op jit(solution)/shard_map/dot_general | solution.py:25
  54.5 1.3 %collective-permute-start.3 = (f32[128,512]{1,0:T(8,128)S(1)}, f32[128,512]{1,0:T(8,128)S(1)}, u32[]{:S(2)}, u32[]{:S(2)}) collective-permute-start(f32[128,512]{1,0:T(8,128)S(1)} %convolution_bitcast_fusion), channel_id=1, source_target_pairs={{0,4},{4,0},{8,12},{12,8},{16,20},{20,16},{24,28},{28,24},{1,5},{5... | collective-permute-start | bytes 786440 | tf_op jit(solution)/shard_map/ppermute | solution.py:10
  55.7 5.2 %collective-permute-done.3 = f32[128,512]{1,0:T(8,128)S(1)} collective-permute-done((f32[128,512]{1,0:T(8,128)S(1)}, f32[128,512]{1,0:T(8,128)S(1)}, u32[]{:S(2)}, u32[]{:S(2)}) %collective-permute-start.3) | collective-permute-done | bytes 262176 | tf_op jit(solution)/shard_map/ppermute | solution.py:10
  60.9 1.3 %collective-permute-start.4 = (f32[128,512]{1,0:T(8,128)S(1)}, f32[128,512]{1,0:T(8,128)S(1)}, u32[]{:S(2)}, u32[]{:S(2)}) collective-permute-start(f32[128,512]{1,0:T(8,128)S(1)} %add.71), channel_id=1, source_target_pairs={{0,8},{4,12},{8,0},{12,4},{16,24},{20,28},{24,16},{28,20},{1,9},{5... | collective-permute-start | bytes 786440 | tf_op jit(solution)/shard_map/ppermute | solution.py:10
  62.3 6.4 %collective-permute-done.4 = f32[128,512]{1,0:T(8,128)S(1)} collective-permute-done((f32[128,512]{1,0:T(8,128)S(1)}, f32[128,512]{1,0:T(8,128)S(1)}, u32[]{:S(2)}, u32[]{:S(2)}) %collective-permute-start.4) | collective-permute-done | bytes 262176 | tf_op jit(solution)/shard_map/ppermute | solution.py:10
  68.7 0.0 copy-done.1
  68.7 3.8 %collective-permute-start.5 = (f32[128,512]{1,0:T(8,128)S(1)}, f32[128,512]{1,0:T(8,128)S(1)}, u32[]{:S(2)}, u32[]{:S(2)}) collective-permute-start(f32[128,512]{1,0:T(8,128)S(1)} %add.72), channel_id=1, source_target_pairs={{0,16},{4,20},{8,24},{12,28},{16,0},{20,4},{24,8},{28,12},{1,17},{... | collective-permute-start | bytes 786440 | tf_op jit(solution)/shard_map/ppermute | solution.py:10
  72.5 7.2 %collective-permute-done.5 = f32[128,512]{1,0:T(8,128)S(1)} collective-permute-done((f32[128,512]{1,0:T(8,128)S(1)}, f32[128,512]{1,0:T(8,128)S(1)}, u32[]{:S(2)}, u32[]{:S(2)}) %collective-permute-start.5) | collective-permute-done | bytes 262176 | tf_op jit(solution)/shard_map/ppermute | solution.py:10
  79.7 1.4 %fusion.12 = f32[128,512]{1,0:T(8,128)S(1)} fusion(f32[128,512]{1,0:T(8,128)S(1)} %collective-permute-done.5, f32[128,512]{1,0:T(8,128)S(1)} %add.72, pred[]{:T(512)S(6)} %eq.15, f32[7,256,256]{2,1,0:T(8,128)} %param.9, s32[]{:T(128)S(6)} %select_n.100, s32[]{:T(128)S(6)} %select_n.103), kind=kOutput, calls=%fused_computation.21 | convolution fusion | flops 201719808 | bytes 917513 | tf_op jit(solution)/shard_map/dot_general | solution.py:45
  81.0 4.9 %bitcast_subtract_fusion = f32[1024,512]{1,0:T(8,128)} fusion(f32[1024,512]{1,0:T(8,128)} %copy-done.1, f32[128,512]{1,0:T(8,128)S(1)} %fusion.12, f32[3,1024,128]{2,1,0:T(8,128)} %param.7), kind=kOutput, calls=%fused_computation | convolution fusion | flops 805830656 | bytes 4980736 | tf_op jit(solution)/shard_map/dot_general | solution.py:48
  (3 shorter events, 0.1 us)
Async XLA Ops:
  0.0 1.6 %copy-start = (f32[1024,512]{1,0:T(8,128)S(1)}, f32[1024,512]{1,0:T(8,128)}, u32[]{:S(2)}) copy-start(f32[1024,512]{1,0:T(8,128)} %param.5) | copy-start | bytes 6291460
  10.4 1.3 %copy-start.3 = (f32[1024,512]{1,0:T(8,128)}, f32[1024,512]{1,0:T(8,128)S(1)}, u32[]{:S(2)}) copy-start(f32[1024,512]{1,0:T(8,128)S(1)} %fusion.45) | copy-start | bytes 6291460
  14.2 9.4 %collective-permute-start = (f32[128,512]{1,0:T(8,128)S(1)}, f32[128,512]{1,0:T(8,128)S(1)}, u32[]{:S(2)}, u32[]{:S(2)}) collective-permute-start(f32[128,512]{1,0:T(8,128)S(1)} %convolution_bitcast_fusion.2), channel_id=1, source_target_pairs={{0,4},{4,0},{8,12},{12,8},{16,20},{20,16},{24,28},{28,24},{1,5},{5... | collective-permute-start | bytes 786440 | tf_op jit(solution)/shard_map/ppermute | solution.py:10
  28.6 1.3 %copy-start.2 = (f32[1024,512]{1,0:T(8,128)}, f32[1024,512]{1,0:T(8,128)S(1)}, u32[]{:S(2)}) copy-start(f32[1024,512]{1,0:T(8,128)S(1)} %bitcast_subtract_fusion.2) | copy-start | bytes 6291460
  32.4 7.5 %collective-permute-start.1 = (f32[128,512]{1,0:T(8,128)S(1)}, f32[128,512]{1,0:T(8,128)S(1)}, u32[]{:S(2)}, u32[]{:S(2)}) collective-permute-start(f32[128,512]{1,0:T(8,128)S(1)} %convolution_bitcast_fusion.1), channel_id=1, source_target_pairs={{0,4},{4,0},{8,12},{12,8},{16,20},{20,16},{24,28},{28,24},{1,5},{5... | collective-permute-start | bytes 786440 | tf_op jit(solution)/shard_map/ppermute | solution.py:10
  39.9 6.7 %collective-permute-start.2 = (f32[128,512]{1,0:T(8,128)S(1)}, f32[128,512]{1,0:T(8,128)S(1)}, u32[]{:S(2)}, u32[]{:S(2)}) collective-permute-start(f32[128,512]{1,0:T(8,128)S(1)} %add.67), channel_id=1, source_target_pairs={{0,8},{4,12},{8,0},{12,4},{16,24},{20,28},{24,16},{28,20},{1,9},{5... | collective-permute-start | bytes 786440 | tf_op jit(solution)/shard_map/ppermute | solution.py:10
  51.6 17.1 %copy-start.1 = (f32[1024,512]{1,0:T(8,128)}, f32[1024,512]{1,0:T(8,128)S(1)}, u32[]{:S(2)}) copy-start(f32[1024,512]{1,0:T(8,128)S(1)} %bitcast_subtract_fusion.1) | copy-start | bytes 6291460
  54.5 6.4 %collective-permute-start.3 = (f32[128,512]{1,0:T(8,128)S(1)}, f32[128,512]{1,0:T(8,128)S(1)}, u32[]{:S(2)}, u32[]{:S(2)}) collective-permute-start(f32[128,512]{1,0:T(8,128)S(1)} %convolution_bitcast_fusion), channel_id=1, source_target_pairs={{0,4},{4,0},{8,12},{12,8},{16,20},{20,16},{24,28},{28,24},{1,5},{5... | collective-permute-start | bytes 786440 | tf_op jit(solution)/shard_map/ppermute | solution.py:10
  60.9 7.7 %collective-permute-start.4 = (f32[128,512]{1,0:T(8,128)S(1)}, f32[128,512]{1,0:T(8,128)S(1)}, u32[]{:S(2)}, u32[]{:S(2)}) collective-permute-start(f32[128,512]{1,0:T(8,128)S(1)} %add.71), channel_id=1, source_target_pairs={{0,8},{4,12},{8,0},{12,4},{16,24},{20,28},{24,16},{28,20},{1,9},{5... | collective-permute-start | bytes 786440 | tf_op jit(solution)/shard_map/ppermute | solution.py:10
  68.7 11.0 %collective-permute-start.5 = (f32[128,512]{1,0:T(8,128)S(1)}, f32[128,512]{1,0:T(8,128)S(1)}, u32[]{:S(2)}, u32[]{:S(2)}) collective-permute-start(f32[128,512]{1,0:T(8,128)S(1)} %add.72), channel_id=1, source_target_pairs={{0,16},{4,20},{8,24},{12,28},{16,0},{20,4},{24,8},{28,12},{1,17},{... | collective-permute-start | bytes 786440 | tf_op jit(solution)/shard_map/ppermute | solution.py:10
where the time goes:
time: 86.4 us; the launch traced here: 85.9 us
  waiting for transfers between devices  35.8 us (41%)
  matrix products  32.8 us (38%)
  starting transfers between devices  12.9 us (15%)
  local copies, waits for them, and re-layouts  4.22 us (5%)
    ppermute x6, waiting for transfers between devices, swapped(): lax.ppermute(x, axis, [(i, i ^ 1 << apart) for i in range(lax.axis_size(a...  35.8 us
    ppermute x6, starting transfers between devices, swapped(): lax.ppermute(x, axis, [(i, i ^ 1 << apart) for i in range(lax.axis_size(a...  12.9 us
    dot_general x3, matrix products, on_device(): jnp.dot(basis_left[level_index - 1], coefficients, precision=highest, pre...  12 us
    dot_general x1, matrix products, on_device(): jnp.dot(leaf_inverse, rhs, precision=highest, preferred_element_type=jnp....  8.81 us
    dot_general x3, matrix products, on_device(): lax.dot_general(basis_right[level_index - 1], current, (((0,), (0,)), (()...  7.83 us
    unnamed x8, local copies, waits for them, and re-layouts  4.22 us
    dot_general x3, matrix products, on_device(): jnp.dot(core_rows, stacked, precision=highest, preferred_element_type=jnp...  4.1 us
  transfers between devices with their start and end apart: 6, of which 6 were waited for; matrix products, arithmetic and copies ran while one was open for 0% of the time, Pallas kernels for 0%

commit v1 on v0

v1 whole, which is shorter than its diff:
```python
import functools

import jax
import jax.numpy as jnp
from jax import lax
from jax.experimental import pallas as pl
from jax.experimental.pallas import tpu as pltpu
from jax.sharding import PartitionSpec as P

F32 = jnp.float32
BF16 = jnp.bfloat16


def swapped(x, axis, apart):
    return lax.ppermute(x, axis, [(i, i ^ 1 << apart) for i in range(lax.axis_size(axis))])


def general(rhs, leaf_inverse, basis_left, basis_right, cores):
    highest = lax.Precision.HIGHEST
    current = jnp.dot(leaf_inverse, rhs, precision=highest, preferred_element_type=F32)
    devices = lax.axis_size("rows")
    tree_depth = devices.bit_length() - 1
    position = lax.axis_index("rows")
    rank_size = basis_left.shape[2]
    for level_index in range(basis_left.shape[0], 0, -1):
        span_devices = devices >> level_index
        child_index = position // span_devices
        node_index = child_index // 2
        half_index = child_index % 2
        child_total = lax.dot_general(
            basis_right[level_index - 1],
            current,
            (((0,), (0,)), ((), ())),
            precision=highest,
            preferred_element_type=F32,
        )
        for bit_number in range(tree_depth - level_index):
            child_total = child_total + swapped(child_total, "rows", bit_number)
        sibling = swapped(child_total, "rows", tree_depth - level_index)
        stacked = jnp.where(
            half_index == 0,
            jnp.concatenate([child_total, sibling], axis=0),
            jnp.concatenate([sibling, child_total], axis=0),
        )
        core_block = lax.dynamic_index_in_dim(
            cores, 2 ** (level_index - 1) - 1 + node_index, 0, keepdims=False
        )
        core_rows = lax.dynamic_slice_in_dim(core_block, half_index * rank_size, rank_size, 0)
        coefficients = jnp.dot(core_rows, stacked, precision=highest, preferred_element_type=F32)
        current = current - jnp.dot(
            basis_left[level_index - 1], coefficients, precision=highest, preferred_element_type=F32
        )
    return current


def split(x):
    high = x.astype(BF16)
    return high, (x - high.astype(F32)).astype(BF16)


def weights(x):
    high, low = split(x)
    return jnp.concatenate([high, high, low], axis=1)


def values(x):
    high, low = split(x)
    return jnp.concatenate([high, low, high], axis=0)


def dot(a, b):
    return jnp.dot(a, b, preferred_element_type=F32)


def kernel(
    rhs_h, leaf_h, left_h, right_h, cores_h, out_h,
    rhs, leaf, left, right, core,
    leaf3, right3, left3, core3, mix3, x3, y3,
    y, proj, mix, up, upmix, top, c3s, c2s,
    in_sem, out_sem, send_y, recv_y, send_z, recv_z, send_t, recv_t,
):
    n, cols = rhs.shape
    rank = left.shape[2]
    chunks, _, _, wide = proj.shape
    me = lax.axis_index("rows")
    bit_y = lax.rem(me, 2)
    bit_z = lax.rem(me // 2, 2)
    bit_t = me // 4
    at_y = me + 1 - 2 * bit_y
    at_z = me + 2 - 4 * bit_z
    at_t = me + 4 - 8 * bit_t

    blocks = 4
    tall = n // blocks
    loads = []

    def load(src, dst):
        copy = pltpu.make_async_copy(src, dst, in_sem.at[len(loads)])
        copy.start()
        loads.append(copy)
        return copy

    load_right = load(right_h, right)
    load_left = load(left_h, left)
    load_rhs = load(rhs_h, rhs)
    load_leaf = [
        load(leaf_h.at[pl.ds(i * tall, tall), :], leaf.at[pl.ds(i * tall, tall), :])
        for i in range(blocks)
    ]
    load_core = [
        load(cores_h.at[3 + me // 2], core.at[2]),
        load(cores_h.at[1 + me // 4], core.at[1]),
        load(cores_h.at[0], core.at[0]),
    ]

    barrier = pltpu.get_barrier_semaphore()
    for other in (at_y, at_z, at_t):
        pl.semaphore_signal(
            barrier, inc=1, device_id={"rows": other}, device_id_type=pl.DeviceIdType.MESH
        )

    sends = []

    def send(ref, slot, other, send_sem, recv_sem, k):
        copy = pltpu.make_async_remote_copy(
            src_ref=ref.at[slot],
            dst_ref=ref.at[slot],
            send_sem=send_sem.at[k],
            recv_sem=recv_sem.at[k],
            device_id={"rows": other},
            device_id_type=pl.DeviceIdType.MESH,
        )
        copy.start()
        sends.append(copy)
        return copy

    load_right.wait()
    for i in range(3):
        right3[pl.ds(i * rank, rank), :] = weights(jnp.transpose(right[2 - i]))
    load_left.wait()
    for i in range(3):
        left3[:, pl.ds(i * 3 * rank, 3 * rank)] = weights(left[2 - i])
    mix[bit_y, pl.ds(0, 2 * rank), :] = dot(right3[pl.ds(rank, 2 * rank), :], values(left[2]))
    mix[bit_y, pl.ds(2 * rank, rank), :] = dot(right3[pl.ds(2 * rank, rank), :], values(left[1]))

    pl.semaphore_wait(barrier, 3)
    mix_y = send(mix, bit_y, at_y, send_y, recv_y, chunks)

    load_rhs.wait()
    for i in range(blocks):
        load_leaf[i].wait()
        leaf3[pl.ds(i * tall, tall), :] = weights(leaf[pl.ds(i * tall, tall), :])
    got_y = [None] * chunks
    half = 2 * wide
    for h in range(cols // half):
        x3[...] = values(rhs[:, pl.ds(h * half, half)])
        product = dot(leaf3[...], x3[...])
        y3[...] = values(product)
        for j in range(2):
            y[2 * h + j] = product[:, j * wide:(j + 1) * wide]
        partial = dot(right3[...], y3[...])
        for j in range(2):
            c = 2 * h + j
            proj[c, bit_y] = partial[:, j * wide:(j + 1) * wide]
            got_y[c] = send(proj.at[c], bit_y, at_y, send_y, recv_y, c)

    for copy in load_core:
        copy.wait()
    for i in range(3):
        core3[i] = weights(core[i])
    mix_y.wait_recv()
    upmix[bit_z] = mix[0, pl.ds(2 * rank, rank), :] + mix[1, pl.ds(2 * rank, rank), :]
    mix_z = send(upmix, bit_z, at_z, send_z, recv_z, chunks)
    mix3[...] = weights(
        jnp.concatenate([mix[0, pl.ds(0, 2 * rank), :], mix[1, pl.ds(0, 2 * rank), :]], axis=1)
    )
    got_z = [None] * chunks
    got_t = [None] * chunks
    upmix3 = []
    outs = []

    def first(c):
        got_y[c].wait_recv()
        stack = jnp.concatenate([proj[c, 0, pl.ds(0, rank), :], proj[c, 1, pl.ds(0, rank), :]], axis=0)
        coeff = dot(core3[2], values(stack))
        rest = proj[c, 0, pl.ds(rank, 2 * rank), :] + proj[c, 1, pl.ds(rank, 2 * rank), :]
        up[c, bit_z] = rest - dot(mix3[...], values(coeff))
        got_z[c] = send(up.at[c], bit_z, at_z, send_z, recv_z, c)
        c3s[0] = coeff[:rank]
        c3s[1] = coeff[rank:]
        y[c] = y[c] - dot(left3[:, pl.ds(0, 3 * rank)], values(c3s[bit_y]))

    def second(c):
        if not upmix3:
            mix_z.wait_recv()
            upmix3.append(weights(jnp.concatenate([upmix[0], upmix[1]], axis=1)))
        got_z[c].wait_recv()
        stack = jnp.concatenate([up[c, 0, pl.ds(0, rank), :], up[c, 1, pl.ds(0, rank), :]], axis=0)
        coeff = dot(core3[1], values(stack))
        rest = up[c, 0, pl.ds(rank, rank), :] + up[c, 1, pl.ds(rank, rank), :]
        top[c, bit_t] = rest - dot(upmix3[0], values(coeff))
        got_t[c] = send(top.at[c], bit_t, at_t, send_t, recv_t, c)
        c2s[0] = coeff[:rank]
        c2s[1] = coeff[rank:]
        y[c] = y[c] - dot(left3[:, pl.ds(3 * rank, 3 * rank)], values(c2s[bit_z]))

    def third(c):
        got_t[c].wait_recv()
        stack = jnp.concatenate([top[c, 0], top[c, 1]], axis=0)
        coeff = dot(core3[0, pl.ds(bit_t * rank, rank), :], values(stack))
        y[c] = y[c] - dot(left3[:, pl.ds(6 * rank, 3 * rank)], values(coeff))
        copy = pltpu.make_async_copy(y.at[c], out_h.at[:, pl.ds(c * wide, wide)], out_sem.at[c])
        copy.start()
        outs.append(copy)

    for step in range(chunks + 3):
        if 0 <= step < chunks:
            first(step)
        if 0 <= step - 1 < chunks:
            second(step - 1)
        if 0 <= step - 2 < chunks:
            third(step - 2)

    for copy in sends:
        copy.wait_send()
    for copy in outs:
        copy.wait()


def on_device(rhs, leaf_inverse, basis_left, basis_right, cores):
    levels, n, rank = basis_left.shape
    cols = rhs.shape[1]
    if levels != 3 or lax.axis_size("rows") != 8 or cols % 256 or n % 1024 or rank % 128:
        return general(rhs, leaf_inverse, basis_left, basis_right, cores)
    wide = 128
    chunks = cols // wide
    any_space = pl.BlockSpec(memory_space=pl.ANY)
    dma = pltpu.SemaphoreType.DMA
    vmem = pltpu.VMEM
    return pl.pallas_call(
        kernel,
        out_shape=jax.ShapeDtypeStruct((n, cols), F32),
        in_specs=[any_space] * 5,
        out_specs=any_space,
        scratch_shapes=[
            vmem((n, cols), F32),
            vmem(leaf_inverse.shape, F32),
            vmem((3, n, rank), F32),
            vmem((3, n, rank), F32),
            vmem((3, 2 * rank, 2 * rank), F32),
            vmem((n, 3 * n), BF16),
            vmem((3 * rank, 3 * n), BF16),
            vmem((n, 9 * rank), BF16),
            vmem((3, 2 * rank, 6 * rank), BF16),
            vmem((2 * rank, 6 * rank), BF16),
            vmem((3 * n, 2 * wide), BF16),
            vmem((3 * n, 2 * wide), BF16),
            vmem((chunks, n, wide), F32),
            vmem((chunks, 2, 3 * rank, wide), F32),
            vmem((2, 3 * rank, rank), F32),
            vmem((chunks, 2, 2 * rank, wide), F32),
            vmem((2, rank, rank), F32),
            vmem((chunks, 2, rank, wide), F32),
            vmem((2, rank, wide), F32),
            vmem((2, rank, wide), F32),
            dma((10,)),
            dma((chunks,)),
            dma((chunks + 1,)),
            dma((chunks + 1,)),
            dma((chunks + 1,)),
            dma((chunks + 1,)),
            dma((chunks,)),
            dma((chunks,)),
        ],
        compiler_params=pltpu.CompilerParams(
            collective_id=0, has_side_effects=True, vmem_limit_bytes=56 * 1024 * 1024
        ),
        name="tree",
    )(rhs, leaf_inverse, basis_left, basis_right, cores)


def solution(mesh):
    placed = (P("rows", "rhs"), P("rows", None), P(None, "rows", None), P(None, "rows", None), P())
    return jax.shard_map(
        on_device, mesh=mesh, in_specs=placed, out_specs=P("rows", "rhs"), check_vma=False
    )
```

time: 86.4 us -> 45.3 us (0.52)
  Pallas kernels: 0 us -> 42.1 us
  waiting for transfers between devices: 35.8 us -> 0 us
  matrix products: 32.8 us -> 0 us
  starting transfers between devices: 12.9 us -> 0 us
  local copies, waits for them, and re-layouts: 4.22 us -> 3.08 us
    pallas_call x0 -> x1, Pallas kernels: none -> 42.1 us  [on_device(): pl.pallas_call(kernel, out_shape=jax.ShapeDtypeStruct((n, cols), F32), in...]
    ppermute x6 -> x0, waiting for transfers between devices: 35.8 us -> none  [swapped(): lax.ppermute(x, axis, [(i, i ^ 1 << apart) for i in range(lax.axis_size(a...]
    dot_general x10 -> x0, matrix products: 32.8 us -> none  [the longest x3 12 us: on_device(): jnp.dot(basis_left[level_index - 1], coefficients, precision=highest, pre...]
    ppermute x6 -> x0, starting transfers between devices: 12.9 us -> none  [swapped(): lax.ppermute(x, axis, [(i, i ^ 1 << apart) for i in range(lax.axis_size(a...]
    unnamed x8 -> x1, local copies, waits for them, and re-layouts: 4.22 us -> 3.08 us
  transfers between devices with their start and end apart: 6 -> 0, of which waited for: 6 -> 0; matrix products, arithmetic and copies ran while one was open for 0% -> 0% of each run, Pallas kernels for 0% -> 0%
where the time goes in v1:
time: 45.3 us; the launch traced here: 45.2 us
  Pallas kernels  42.1 us (93%)
  local copies, waits for them, and re-layouts  3.08 us (7%)
    pallas_call x1, Pallas kernels, on_device(): pl.pallas_call(kernel, out_shape=jax.ShapeDtypeStruct((n, cols), F32), in...  42.1 us
    unnamed x1, local copies, waits for them, and re-layouts  3.08 us

profile of v1, /device:TPU:0, one launch (start us, length us, event | category | flops | bytes accessed | tf_op | source)
XLA Modules:
  0.0 45.2 jit_solution(16519036041919058639)
XLA Ops:
  0.0 42.1 %tree.1 = f32[1024,512]{1,0:T(8,128)} custom-call(f32[1024,512]{1,0:T(8,128)} %rhs_h.1, f32[1024,1024]{1,0:T(8,128)} %leaf_h.1, f32[3,1024,128]{2,1,0:T(8,128)} %left_h.1, f32[3,1024,128]{2,1,0:T(8,128)} %right_h.1, f32[7,256,256]{2,1,0:T(8,128)} %cores_h.1), custom_call_target="tpu_custom_call" | custom-call | tf_op jit(solution)/shard_map/tree/pallas_call | solution.py:240
  42.1 3.1 %copy.7 = f32[1024,512]{1,0:T(8,128)} copy(f32[1024,512]{1,0:T(8,128)} %tree.1) | data formatting | bytes 4194304

commit v2 on v1

v2 whole, which is shorter than its diff:
```python
import jax
import jax.numpy as jnp
from jax import lax
from jax.experimental import pallas as pl
from jax.experimental.pallas import tpu as pltpu
from jax.sharding import PartitionSpec as P

F32 = jnp.float32
BF16 = jnp.bfloat16


def swapped(x, axis, apart):
    return lax.ppermute(x, axis, [(i, i ^ 1 << apart) for i in range(lax.axis_size(axis))])


def general(rhs, leaf_inverse, basis_left, basis_right, cores):
    highest = lax.Precision.HIGHEST
    current = jnp.dot(leaf_inverse, rhs, precision=highest, preferred_element_type=F32)
    devices = lax.axis_size("rows")
    tree_depth = devices.bit_length() - 1
    position = lax.axis_index("rows")
    rank_size = basis_left.shape[2]
    for level_index in range(basis_left.shape[0], 0, -1):
        span_devices = devices >> level_index
        child_index = position // span_devices
        node_index = child_index // 2
        half_index = child_index % 2
        child_total = lax.dot_general(
            basis_right[level_index - 1],
            current,
            (((0,), (0,)), ((), ())),
            precision=highest,
            preferred_element_type=F32,
        )
        for bit_number in range(tree_depth - level_index):
            child_total = child_total + swapped(child_total, "rows", bit_number)
        sibling = swapped(child_total, "rows", tree_depth - level_index)
        stacked = jnp.where(
            half_index == 0,
            jnp.concatenate([child_total, sibling], axis=0),
            jnp.concatenate([sibling, child_total], axis=0),
        )
        core_block = lax.dynamic_index_in_dim(
            cores, 2 ** (level_index - 1) - 1 + node_index, 0, keepdims=False
        )
        core_rows = lax.dynamic_slice_in_dim(core_block, half_index * rank_size, rank_size, 0)
        coefficients = jnp.dot(core_rows, stacked, precision=highest, preferred_element_type=F32)
        current = current - jnp.dot(
            basis_left[level_index - 1], coefficients, precision=highest, preferred_element_type=F32
        )
    return current


def split(x):
    high = x.astype(BF16)
    return high, (x - high.astype(F32)).astype(BF16)


def weights(x):
    high, low = split(x)
    return jnp.concatenate([high, high, low], axis=1)


def values(x):
    high, low = split(x)
    return jnp.concatenate([high, low, high], axis=0)


def dot(a, b):
    return jnp.dot(a, b, preferred_element_type=F32)


def kernel(
    rhs_h, leaf_h, left_h, right_h, cores_h, out_h,
    rhs, leaf, left, right, core,
    leaf3, right3, left3, core3, x3, y3, coeff3,
    y, rest, own3, low2, low1, pair2, pair1, top, mix, upmix, c2s,
    in_sem, out_sem, send_sem, recv_sem,
):
    n, cols = rhs.shape
    rank = left.shape[2]
    chunks, _, _, wide = own3.shape
    half = x3.shape[1]
    me = lax.axis_index("rows")
    bit_y = lax.rem(me, 2)
    bit_z = lax.rem(me // 2, 2)
    bit_t = me // 4
    at_y = me + 1 - 2 * bit_y
    at_z = me + 2 - 4 * bit_z
    at_t = me + 4 - 8 * bit_t

    blocks = 4
    tall = n // blocks
    loads = []

    def load(src, dst):
        copy = pltpu.make_async_copy(src, dst, in_sem.at[len(loads)])
        copy.start()
        loads.append(copy)
        return copy

    load_right = load(right_h, right)
    load_left = load(left_h, left)
    load_rhs = load(rhs_h, rhs)
    load_leaf = [
        load(leaf_h.at[pl.ds(i * tall, tall), :], leaf.at[pl.ds(i * tall, tall), :])
        for i in range(blocks)
    ]
    load_core = [
        load(cores_h.at[3 + me // 2], core.at[2]),
        load(cores_h.at[1 + me // 4], core.at[1]),
        load(cores_h.at[0], core.at[0]),
    ]

    barrier = pltpu.get_barrier_semaphore()
    for other in (at_y, at_z, at_t):
        pl.semaphore_signal(
            barrier, inc=1, device_id={"rows": other}, device_id_type=pl.DeviceIdType.MESH
        )

    sends = []

    def send(ref, slot, other):
        k = len(sends)
        copy = pltpu.make_async_remote_copy(
            src_ref=ref.at[slot],
            dst_ref=ref.at[slot],
            send_sem=send_sem.at[k],
            recv_sem=recv_sem.at[k],
            device_id={"rows": other},
            device_id_type=pl.DeviceIdType.MESH,
        )
        copy.start()
        sends.append(copy)
        return copy

    load_right.wait()
    for i in range(3):
        right3[pl.ds(i * rank, rank), :] = weights(jnp.transpose(right[2 - i]))
    load_left.wait()
    mix[bit_y] = dot(right3[pl.ds(2 * rank, rank), :], values(left[1]))
    pl.semaphore_wait(barrier, 3)
    mix_y = send(mix, bit_y, at_y)
    mix3 = weights(dot(right3[pl.ds(rank, 2 * rank), :], values(left[2])))
    for i in range(3):
        left3[:, pl.ds(i * 3 * rank, 3 * rank)] = weights(left[2 - i])

    pieces = 2
    deep = n // pieces
    got = {}
    outs = []

    def leaf_piece(h, i):
        if i == 0:
            if h == 0:
                load_rhs.wait()
            x3[...] = values(rhs[:, pl.ds(h * half, half)])
        if h == 0:
            for j in range(i * blocks // pieces, (i + 1) * blocks // pieces):
                load_leaf[j].wait()
                leaf3[pl.ds(j * tall, tall), :] = weights(leaf[pl.ds(j * tall, tall), :])
        product = dot(leaf3[pl.ds(i * deep, deep), :], x3[...])
        high, low = split(product)
        y3[pl.ds(i * deep, deep), :] = high
        y3[pl.ds(n + i * deep, deep), :] = low
        y3[pl.ds(2 * n + i * deep, deep), :] = high
        for j in range(half // wide):
            y[h * half // wide + j, pl.ds(i * deep, deep), :] = product[:, j * wide:(j + 1) * wide]

    def project(h):
        partial = dot(right3[...], y3[...])
        for j in range(half // wide):
            c = h * half // wide + j
            own3[c, bit_y] = partial[:rank, j * wide:(j + 1) * wide]
            got["a", c] = send(own3.at[c], bit_y, at_y)
            rest[c] = partial[rank:, j * wide:(j + 1) * wide]

    def small():
        for copy in load_core:
            copy.wait()
        for i in range(3):
            core3[i] = weights(core[i])

    def middle():
        mix_y.wait_recv()
        upmix[bit_z] = mix[0] + mix[1]
        got["m"] = send(upmix, bit_z, at_z)

    def stack(ref, c):
        return values(jnp.concatenate([ref[c, 0], ref[c, 1]], axis=0))

    def third_level(c):
        got["a", c].wait_recv()
        coeff = values(dot(core3[2, pl.ds(bit_y * rank, rank), :], stack(own3, c)))
        reduced = rest[c] - dot(mix3, coeff)
        low2[c, bit_y] = reduced[:rank]
        got["b", c] = send(low2.at[c], bit_y, at_y)
        low1[c, bit_z] = reduced[rank:]
        got["c", c] = send(low1.at[c], bit_z, at_z)
        coeff3[c, pl.ds(0, 3 * rank), :] = coeff

    def pairs(c):
        got["b", c].wait_recv()
        pair2[c, bit_z] = low2[c, 0] + low2[c, 1]
        got["d", c] = send(pair2.at[c], bit_z, at_z)
        got["c", c].wait_recv()
        pair1[c, bit_y] = low1[c, 0] + low1[c, 1]
        got["e", c] = send(pair1.at[c], bit_y, at_y)

    def second_level(c):
        if "m3" not in got:
            got["m"].wait_recv()
            got["m3"] = weights(jnp.concatenate([upmix[0], upmix[1]], axis=1))
        got["d", c].wait_recv()
        coeff = dot(core3[1], stack(pair2, c))
        got["e", c].wait_recv()
        top[c, bit_t] = pair1[c, 0] + pair1[c, 1] - dot(got["m3"], values(coeff))
        got["f", c] = send(top.at[c], bit_t, at_t)
        c2s[0] = coeff[:rank]
        c2s[1] = coeff[rank:]
        coeff3[c, pl.ds(3 * rank, 3 * rank), :] = values(c2s[bit_z])
        y[c] = y[c] - dot(left3[:, pl.ds(0, 6 * rank)], coeff3[c])

    def first_level(c):
        got["f", c].wait_recv()
        coeff = values(dot(core3[0, pl.ds(bit_t * rank, rank), :], stack(top, c)))
        y[c] = y[c] - dot(left3[:, pl.ds(6 * rank, 3 * rank)], coeff)
        copy = pltpu.make_async_copy(y.at[c], out_h.at[:, pl.ds(c * wide, wide)], out_sem.at[c])
        copy.start()
        outs.append(copy)

    last = cols // half - 1
    per = half // wide
    for i in range(pieces):
        leaf_piece(0, i)
    project(0)
    small()
    for h in range(1, last + 1):
        before = range((h - 1) * per, h * per)
        leaf_piece(h, 0)
        if h == 1:
            middle()
        for c in before:
            third_level(c)
        for i in range(1, pieces):
            leaf_piece(h, i)
        project(h)
        for c in before:
            pairs(c)
    for c in range(last * per, chunks):
        third_level(c)
    ready = last * per
    for c in range(ready):
        second_level(c)
        if ready + c < chunks:
            pairs(ready + c)
    for c in range(ready + min(ready, per), chunks):
        pairs(c)
    for c in range(ready):
        first_level(c)
    for c in range(ready, chunks):
        second_level(c)
    for c in range(ready, chunks):
        first_level(c)

    for copy in sends:
        copy.wait_send()
    for copy in outs:
        copy.wait()


def on_device(rhs, leaf_inverse, basis_left, basis_right, cores):
    levels, n, rank = basis_left.shape
    cols = rhs.shape[1]
    if levels != 3 or lax.axis_size("rows") != 8 or cols % 512 or n % 1024 or rank % 128:
        return general(rhs, leaf_inverse, basis_left, basis_right, cores)
    wide = 128
    half = 256
    chunks = cols // wide
    hbm = pl.BlockSpec(memory_space=pltpu.HBM)
    dma = pltpu.SemaphoreType.DMA
    vmem = pltpu.VMEM
    swap = vmem((chunks, 2, rank, wide), F32)
    return pl.pallas_call(
        kernel,
        out_shape=pltpu.VMEM((n, cols), F32),
        in_specs=[hbm] * 5,
        out_specs=pl.BlockSpec(memory_space=pl.ANY),
        scratch_shapes=[
            vmem((n, cols), F32),
            vmem(leaf_inverse.shape, F32),
            vmem((3, n, rank), F32),
            vmem((3, n, rank), F32),
            vmem((3, 2 * rank, 2 * rank), F32),
            vmem((n, 3 * n), BF16),
            vmem((3 * rank, 3 * n), BF16),
            vmem((n, 9 * rank), BF16),
            vmem((3, 2 * rank, 6 * rank), BF16),
            vmem((3 * n, half), BF16),
            vmem((3 * n, half), BF16),
            vmem((chunks, 6 * rank, wide), BF16),
            vmem((chunks, n, wide), F32),
            vmem((chunks, 2 * rank, wide), F32),
            swap, swap, swap, swap, swap, swap,
            vmem((2, rank, rank), F32),
            vmem((2, rank, rank), F32),
            vmem((2, rank, wide), F32),
            dma((10,)),
            dma((chunks,)),
            dma((6 * chunks + 2,)),
            dma((6 * chunks + 2,)),
        ],
        compiler_params=pltpu.CompilerParams(
            collective_id=0, has_side_effects=True, vmem_limit_bytes=63000 * 1024
        ),
        name="tree",
    )(rhs, leaf_inverse, basis_left, basis_right, cores)


def solution(mesh):
    placed = (P("rows", "rhs"), P("rows", None), P(None, "rows", None), P(None, "rows", None), P())
    return jax.shard_map(
        on_device, mesh=mesh, in_specs=placed, out_specs=P("rows", "rhs"), check_vma=False
    )
```

time: 45.3 us -> 41.5 us (0.916)
  Pallas kernels: 42.1 us -> 40 us
  local copies, waits for them, and re-layouts: 3.08 us -> 1.32 us
    pallas_call x1, Pallas kernels: 42.1 us -> 40 us  [on_device(): pl.pallas_call(kernel, out_shape=pltpu.VMEM((n, cols), F32), in_specs=[hb...]
    unnamed x1, local copies, waits for them, and re-layouts: 3.08 us -> 1.32 us
where the time goes in v2:
time: 41.5 us; the launch traced here: 41.3 us
  Pallas kernels  40 us (96%)
  local copies, waits for them, and re-layouts  1.32 us (3%)
    pallas_call x1, Pallas kernels, on_device(): pl.pallas_call(kernel, out_shape=pltpu.VMEM((n, cols), F32), in_specs=[hb...  40 us
    unnamed x1, local copies, waits for them, and re-layouts  1.32 us

profile of v2, /device:TPU:0, one launch (start us, length us, event | category | flops | bytes accessed | tf_op | source)
XLA Modules:
  0.0 41.3 jit_solution(14153141606562802046)
XLA Ops:
  0.0 40.0 %tree.1 = f32[1024,512]{1,0:T(8,128)S(1)} custom-call(f32[1024,512]{1,0:T(8,128)} %rhs_h.1, f32[1024,1024]{1,0:T(8,128)} %leaf_h.1, f32[3,1024,128]{2,1,0:T(8,128)} %left_h.1, f32[3,1024,128]{2,1,0:T(8,128)} %right_h.1, f32[7,256,256]{2,1,0:T(8,128)} %cores_h.1), custom_call_target="tpu_custom_call" | custom-call | tf_op jit(solution)/shard_map/tree/pallas_call | solution.py:284
  40.0 1.3 %copy.7 = f32[1024,512]{1,0:T(8,128)} copy(f32[1024,512]{1,0:T(8,128)S(1)} %tree.1) | data formatting | bytes 4194304

commit v3 on v2

--- a/solution.py
+++ b/solution.py
@@ -99,13 +99,13 @@
         loads.append(copy)
         return copy
 
-    load_right = load(right_h, right)
-    load_left = load(left_h, left)
     load_rhs = load(rhs_h, rhs)
     load_leaf = [
         load(leaf_h.at[pl.ds(i * tall, tall), :], leaf.at[pl.ds(i * tall, tall), :])
         for i in range(blocks)
     ]
+    load_right = load(right_h, right)
+    load_left = load(left_h, left)
     load_core = [
         load(cores_h.at[3 + me // 2], core.at[2]),
         load(cores_h.at[1 + me // 4], core.at[1]),
@@ -133,17 +133,6 @@
         copy.start()
         sends.append(copy)
         return copy
-
-    load_right.wait()
-    for i in range(3):
-        right3[pl.ds(i * rank, rank), :] = weights(jnp.transpose(right[2 - i]))
-    load_left.wait()
-    mix[bit_y] = dot(right3[pl.ds(2 * rank, rank), :], values(left[1]))
-    pl.semaphore_wait(barrier, 3)
-    mix_y = send(mix, bit_y, at_y)
-    mix3 = weights(dot(right3[pl.ds(rank, 2 * rank), :], values(left[2])))
-    for i in range(3):
-        left3[:, pl.ds(i * 3 * rank, 3 * rank)] = weights(left[2 - i])
 
     pieces = 2
     deep = n // pieces
@@ -168,6 +157,11 @@
             y[h * half // wide + j, pl.ds(i * deep, deep), :] = product[:, j * wide:(j + 1) * wide]
 
     def project(h):
+        if h == 0:
+            load_right.wait()
+            for i in range(3):
+                right3[pl.ds(i * rank, rank), :] = weights(jnp.transpose(right[2 - i]))
+            pl.semaphore_wait(barrier, 3)
         partial = dot(right3[...], y3[...])
         for j in range(half // wide):
             c = h * half // wide + j
@@ -176,13 +170,22 @@
             rest[c] = partial[rank:, j * wide:(j + 1) * wide]
 
     def small():
+        load_left.wait()
+        got["mix3"] = weights(dot(right3[pl.ds(rank, 2 * rank), :], values(left[2])))
+        mix[bit_y] = dot(right3[pl.ds(2 * rank, rank), :], values(left[1]))
+        got["n"] = send(mix, bit_y, at_y)
         for copy in load_core:
             copy.wait()
+        core3[2] = weights(core[2])
+
+    def prepare():
+        for i in range(2):
+            core3[i] = weights(core[i])
         for i in range(3):
-            core3[i] = weights(core[i])
+            left3[:, pl.ds(i * 3 * rank, 3 * rank)] = weights(left[2 - i])
 
     def middle():
-        mix_y.wait_recv()
+        got["n"].wait_recv()
         upmix[bit_z] = mix[0] + mix[1]
         got["m"] = send(upmix, bit_z, at_z)
 
@@ -192,7 +195,7 @@
     def third_level(c):
         got["a", c].wait_recv()
         coeff = values(dot(core3[2, pl.ds(bit_y * rank, rank), :], stack(own3, c)))
-        reduced = rest[c] - dot(mix3, coeff)
+        reduced = rest[c] - dot(got["mix3"], coeff)
         low2[c, bit_y] = reduced[:rank]
         got["b", c] = send(low2.at[c], bit_y, at_y)
         low1[c, bit_z] = reduced[rank:]
@@ -219,6 +222,8 @@
         c2s[0] = coeff[:rank]
         c2s[1] = coeff[rank:]
         coeff3[c, pl.ds(3 * rank, 3 * rank), :] = values(c2s[bit_z])
+
+    def update(c):
         y[c] = y[c] - dot(left3[:, pl.ds(0, 6 * rank)], coeff3[c])
 
     def first_level(c):
@@ -238,15 +243,17 @@
     for h in range(1, last + 1):
         before = range((h - 1) * per, h * per)
         leaf_piece(h, 0)
-        if h == 1:
-            middle()
         for c in before:
             third_level(c)
         for i in range(1, pieces):
             leaf_piece(h, i)
         project(h)
+        if h == 1:
+            middle()
         for c in before:
             pairs(c)
+        if h == 1:
+            prepare()
     for c in range(last * per, chunks):
         third_level(c)
     ready = last * per
@@ -257,10 +264,12 @@
     for c in range(ready + min(ready, per), chunks):
         pairs(c)
     for c in range(ready):
-        first_level(c)
+        update(c)
     for c in range(ready, chunks):
         second_level(c)
     for c in range(ready, chunks):
+        update(c)
+    for c in range(chunks):
         first_level(c)
 
     for copy in sends:

time: 41.5 us -> 41.4 us (level)
  no operation moved by 1% of the time
where the time goes in v3:
time: 41.4 us; the launch traced here: 41.2 us
  Pallas kernels  39.9 us (96%)
  local copies, waits for them, and re-layouts  1.32 us (3%)
    pallas_call x1, Pallas kernels, on_device(): pl.pallas_call(kernel, out_shape=pltpu.VMEM((n, cols), F32), in_specs=[hb...  39.9 us
    unnamed x1, local copies, waits for them, and re-layouts  1.32 us

profile of v3, /device:TPU:0, one launch (start us, length us, event | category | flops | bytes accessed | tf_op | source)
XLA Modules:
  0.0 41.2 jit_solution(8740667993171183382)
XLA Ops:
  0.0 39.9 %tree.1 = f32[1024,512]{1,0:T(8,128)S(1)} custom-call(f32[1024,512]{1,0:T(8,128)} %rhs_h.1, f32[1024,1024]{1,0:T(8,128)} %leaf_h.1, f32[3,1024,128]{2,1,0:T(8,128)} %left_h.1, f32[3,1024,128]{2,1,0:T(8,128)} %right_h.1, f32[7,256,256]{2,1,0:T(8,128)} %cores_h.1), custom_call_target="tpu_custom_call" | custom-call | tf_op jit(solution)/shard_map/tree/pallas_call | solution.py:293
  39.9 1.3 %copy.7 = f32[1024,512]{1,0:T(8,128)} copy(f32[1024,512]{1,0:T(8,128)S(1)} %tree.1) | data formatting | bytes 4194304
